TPU v7x, 256 devices: a whole 4x4x8 slice. The times are simulated.
256 devices in a mesh: front: 8 (over z), row: 4 (over x_hi, core), col: 8 (over x_lo, y).
Axes of the slice: x: 4 (x_hi: 2, x_lo: 2; x = x_hi * 2 + x_lo), y: 4, z: 8, core: 2. Of those that a mesh axis runs over, the one named last changes fastest.
Arguments:
- front_slab: bfloat16 [8, 2048, 8192], P('front', 'row', 'col'), may hold values from -0.0625 to 0.0625
- samples: bfloat16 [8192, 256], P(('row', 'col')), may hold values from -6 to 6
- child_tiles: bfloat16 [512, 128, 2048], P(('front', 'row', 'col')), may hold values from -0.0625 to 0.0625
- parent_front: int32 [512, 1], P(('front', 'row', 'col')), may hold values from 0 to 7; in each aligned block of 2 rows (0 to 1, 2 to 3, ...) at most 2 rows name the same one
- parent_tile: int32 [512], P(('front', 'row', 'col')), may hold values from 0 to 15
- column_tiles: int32 [512, 16], P(('front', 'row', 'col')), may hold values from 0 to 63
- ranks: int32 [8, 4], P('front', 'row'), may hold values from 128 to 256
Outputs:
- sampled: float32 [8, 2048, 256], P('front', ('row', 'col'))
- bases: float32 [8, 2048, 256], P('front', ('row', 'col'))
Inputs may be any that keep to these rules, and one draw needn't show every extreme that they name: `parent_front`: among the 2 tiles of one device, at most 2 name the same parent front.
All inputs are finite; a program needn't handle non-finite values.
Results may differ from a plain program's by a relative error of at most 0.0003.
Values may be sent and summed in bfloat16 or wider, within the bound.
No kernel may reach another device: no remote copies, remote signals or barrier semaphores. Data moves between devices by JAX's collectives and lax.ppermute only.
A program may use at most 64 MiB of HBM per device.

v0:
```python
import math
import jax
import jax.numpy as jnp
from jax import lax
from jax.sharding import PartitionSpec as P


def in_blocks(x, dim, devices):
    before, after = (x.shape[:dim], x.shape[dim + 1 :])
    return jnp.moveaxis(x.reshape(*before, devices, -1, *after), dim, 0)


def summed_on_arrival(x, axis, dim):
    devices = lax.axis_size(axis)
    pieces = lax.all_to_all(in_blocks(x, dim, devices), axis, 0, 0, tiled=True)
    return jnp.sum(pieces, axis=0)


def in_one_piece(arrays, axis, split_dim, concat_dim, along):
    widths = [math.prod(a.shape[along:]) for a in arrays]
    both = jnp.concatenate(
        [a.reshape(*a.shape[:along], w) for a, w in zip(arrays, widths)], axis=along
    )
    out = lax.all_to_all(both, axis, split_axis=split_dim, concat_axis=concat_dim, tiled=True)
    pieces = jnp.split(out, [sum(widths[:k]) for k in range(1, len(widths))], axis=along)
    return tuple((b.reshape(*out.shape[:along], *a.shape[along:]) for a, b in zip(arrays, pieces)))


def sent_to_all(x, axis):
    copies = jnp.broadcast_to(x, (lax.axis_size(axis), *x.shape))
    return lax.all_to_all(copies, axis, split_axis=0, concat_axis=0, tiled=True)


def taken_together(x, axis):
    everything = sent_to_all(x, axis)
    return jnp.sum(everything, axis=0)


def on_device(front_slab, samples, child_tiles, parent_front, parent_tile, column_tiles, ranks):
    width = samples.shape[1]
    slab = front_slab[0]
    col_width = slab.shape[1]
    omega = lax.all_gather(samples, ("row", "col"), axis=0, tiled=True)
    full = omega.shape[0]
    own = lax.dynamic_slice_in_dim(omega, lax.axis_index("col") * col_width, col_width, 0)
    direct = summed_on_arrival(jnp.dot(slab, own, preferred_element_type=jnp.float32), "col", 0)
    tile_count = child_tiles.shape[0]
    blocks = child_tiles.shape[2] // 128
    omega_tiles = omega.reshape(full // 128, 128, width)
    chosen = omega_tiles[column_tiles]
    pieces = child_tiles.reshape(tile_count, 128, blocks, 128)
    product = jnp.einsum("trkc,tkcs->trs", pieces, chosen, preferred_element_type=jnp.float32)
    parents = lax.axis_size("front")
    row_tiles = slab.shape[0] * lax.axis_size("row") // 128
    dest = parent_front[:, 0]
    capacity = max(2, 2 * ((tile_count + parents - 1) // parents))
    match = (dest[:, None] == jnp.arange(parents, dtype=jnp.int32)[None, :]).astype(jnp.int32)
    before = jnp.cumsum(match, axis=0) - match
    slot = dest * capacity + jnp.sum(before * match, axis=1)
    place = (slot[:, None] == jnp.arange(parents * capacity, dtype=jnp.int32)[None, :]).astype(
        jnp.float32
    )
    sent = jnp.einsum("tq,trs->qrs", place, product, precision=lax.Precision.HIGHEST)
    sent = sent.reshape(parents, capacity, 128, width)
    labels = (
        jnp.dot(parent_tile.astype(jnp.float32) + 1.0, place, precision=lax.Precision.HIGHEST) - 1.0
    )
    labels = labels.reshape(parents, capacity)
    arrived, arrived_labels = in_one_piece((sent, labels), "front", 0, 0, 2)
    tile_index = arrived_labels.reshape(-1).astype(jnp.int32)
    spread = (tile_index[:, None] == jnp.arange(row_tiles, dtype=jnp.int32)[None, :]).astype(
        jnp.float32
    )
    gathered = arrived.reshape(parents * capacity, 128, width)
    rows_full = jnp.einsum("qj,qrs->jrs", spread, gathered, precision=lax.Precision.HIGHEST)
    rows_full = rows_full.reshape(row_tiles * 128, width)
    extended = summed_on_arrival(rows_full, ("row", "col"), 0)
    sampled = direct + extended
    mask = (jnp.arange(width, dtype=jnp.int32) < ranks[0, 0]).astype(jnp.float32)
    masked = sampled * mask[None, :]
    partial_gram = jnp.dot(masked.T, masked, precision=lax.Precision.HIGHEST)
    gram = taken_together(partial_gram, "col") + jnp.diag(1.0 - mask)
    lower = jnp.linalg.cholesky(gram)
    basis = lax.linalg.triangular_solve(
        lower, masked, left_side=False, lower=True, transpose_a=True
    )
    return (sampled[None], basis[None])


def solution(mesh):
    in_specs = (
        P("front", "row", "col"),
        P(("row", "col"), None),
        P(("front", "row", "col"), None, None),
        P(("front", "row", "col"), None),
        P(("front", "row", "col")),
        P(("front", "row", "col"), None),
        P("front", "row"),
    )
    out_specs = (P("front", ("row", "col"), None), P("front", ("row", "col"), None))
    return jax.shard_map(
        on_device, mesh=mesh, in_specs=in_specs, out_specs=out_specs, check_vma=False
    )
```

profile of v0, /device:TPU:1, one launch (start us, length us, event | category | flops | bytes accessed | tf_op | source)
XLA Modules:
  0.0 331.1 jit_solution(624082861867423095)
XLA Ops:
  7.9 0.7 fusion.22
  8.7 0.8 select_reduce_fusion.2
  10.2 0.8 fusion.2
  11.9 90.9 %all-gather.2.cloned.1.call-done = bf16[8192,256]{1,0:T(8,128)(2,1)} async-done(((bf16[256,256]{1,0:T(8,128)(2,1)}), bf16[8192,256]{1,0:T(8,128)(2,1)}) %all-gather.2.cloned.1.call-update) | async-done | bytes 4194320 | tf_op jit(solution)/shard_map/all_gather | solution.py:43
  102.8 2.9 gather_fusion
  105.7 2.1 convolution_bitcast_fusion.1
  108.0 1.2 fusion.20
  109.1 2.5 copy.20
  111.7 2.7 reshape_reshape.13
  114.3 2.3 pad_maximum_fusion
  116.7 7.5 %all-to-all-start.1 = ((f32[8,2,32769]{2,1,0:T(2,128)}), f32[8,2,32769]{2,1,0:T(2,128)S(1)}, u32[]{:S(2)}, u32[]{:S(2)}) async-start(f32[8,2,32769]{2,1,0:T(2,128)} %pad_maximum_fusion), calls=%async_computation.1 | async-start | bytes 4210688 | tf_op jit(solution)/shard_map/all_to_all | solution.py:24
  124.2 2.3 convolution_bitcast_fusion
  126.5 2.0 copy.16
  128.6 47.6 %all-to-all-done.1 = f32[8,2,32769]{2,1,0:T(2,128)S(1)} async-done(((f32[8,2,32769]{2,1,0:T(2,128)}), f32[8,2,32769]{2,1,0:T(2,128)S(1)}, u32[]{:S(2)}, u32[]{:S(2)}) %all-to-all-start.1) | async-done | bytes 2097248 | tf_op jit(solution)/shard_map/all_to_all | solution.py:24
  176.2 4.2 %all-to-all-start = ((f32[8,64,256]{2,1,0:T(8,128)}), f32[8,64,256]{2,1,0:T(8,128)}, u32[]{:S(2)}, u32[]{:S(2)}) async-start(f32[8,64,256]{2,1,0:T(8,128)} %bitcast.87), calls=%async_computation | async-start | bytes 1048576 | tf_op jit(solution)/shard_map/all_to_all | solution.py:15
  180.3 1.5 split.9
  181.8 4.0 %reshape_reshape.15 = f32[16,128,256]{2,1,0:T(8,128)} reshape(f32[8,2,32768]{2,1,0:T(2,128)} %split.9) | data formatting | bytes 4194304 | tf_op jit(solution)/shard_map/reshape;reshape | solution.py:74
  186.1 3.8 %fusion = f32[16,128,256]{2,0,1:T(8,128)S(1)} fusion(f32[16,128,256]{2,1,0:T(8,128)} %reshape_reshape.15, s32[16]{0:T(128)S(1)} %convert_element_type.32), kind=kOutput, calls=%fused_computation.4 | convolution fusion | flops 100663552 | bytes 4194368 | tf_op jit(solution)/shard_map/qj,qrs->jrs/dot_general | solution.py:75
  189.9 2.6 copy.23
  192.5 8.3 %all-to-all-start.2 = ((f32[32,64,256]{2,1,0:T(8,128)}), f32[32,64,256]{2,1,0:T(8,128)S(1)}, u32[]{:S(2)}, u32[]{:S(2)}) async-start(f32[32,64,256]{2,1,0:T(8,128)} %bitcast.15), calls=%async_computation.2 | async-start | bytes 4194304 | tf_op jit(solution)/shard_map/all_to_all | solution.py:15
  201.4 1.1 reduce_sum.40
  202.5 25.7 %all-to-all-done.2 = f32[32,64,256]{2,1,0:T(8,128)S(1)} async-done(((f32[32,64,256]{2,1,0:T(8,128)}), f32[32,64,256]{2,1,0:T(8,128)S(1)}, u32[]{:S(2)}, u32[]{:S(2)}) %all-to-all-start.2) | async-done | bytes 2097184 | tf_op jit(solution)/shard_map/all_to_all | solution.py:15
  229.4 1.5 broadcast_in_dim.39
  230.9 3.8 %all-to-all-start.3 = ((f32[8,256,256]{2,1,0:T(8,128)}), f32[8,256,256]{2,1,0:T(8,128)S(1)}, u32[]{:S(2)}, u32[]{:S(2)}) async-start(f32[8,256,256]{2,1,0:T(8,128)} %broadcast_in_dim.39), calls=%async_computation.3 | async-start | bytes 4194304 | tf_op jit(solution)/shard_map/all_to_all | solution.py:31
  234.7 26.1 %all-to-all-done.3 = f32[8,256,256]{2,1,0:T(8,128)S(1)} async-done(((f32[8,256,256]{2,1,0:T(8,128)}), f32[8,256,256]{2,1,0:T(8,128)S(1)}, u32[]{:S(2)}, u32[]{:S(2)}) %all-to-all-start.3) | async-done | bytes 2097184 | tf_op jit(solution)/shard_map/all_to_all | solution.py:31
  261.2 11.7 %cholesky.49 = f32[128,128]{1,0:T(8,128)S(1)} custom-call(f32[128,128]{1,0:T(8,128)S(1)} %cholesky.115), custom_call_target="Cholesky" | custom-call | tf_op jit(solution)/shard_map/jit(cholesky)/cholesky | solution.py:83
  273.0 9.8 %custom-call.14 = f32[1,128,128]{1,2,0:T(8,128)S(1)} custom-call(f32[1,128,128]{2,1,0:T(8,128)S(1)} %get-tuple-element.25), custom_call_target="InvertDiagBlocksLowerTriangular" | custom-call | tf_op jit(solution)/shard_map/jit(cholesky)/cholesky | solution.py:83
  283.3 11.7 %cholesky.103 = f32[128,128]{1,0:T(8,128)S(1)} custom-call(f32[128,128]{1,0:T(8,128)S(1)} %convolution_subtract_fusion), custom_call_target="Cholesky" | custom-call | tf_op jit(solution)/shard_map/jit(cholesky)/cholesky | solution.py:83
  297.2 5.3 %while.1 = (s32[]{:T(128)}, f32[256,256]{1,0:T(8,128)S(1)}, s32[2,2]{1,0:T(2,128)S(1)}, f32[2,128,128]{2,1,0:T(8,128)}, s32[]{:T(128)}) while((s32[]{:T(128)}, f32[256,256]{1,0:T(8,128)S(1)}, s32[2,2]{1,0:T(2,128)S(1)}, f32[2,128,128]{2,1,0:T(8,128)}, s32[]{:T(128)}) %tuple.28), condition=%wide.while_cond, body=%wide.while_body.sunk | while | flops 2 | bytes 132205 | solution.py:84
  297.8 2.0 bitcast_dynamic-update-slice_fusion.2
  300.4 2.0 bitcast_dynamic-update-slice_fusion.2
  302.5 20.5 %custom-call.15 = f32[2,128,128]{1,2,0:T(8,128)S(1)} custom-call(f32[2,128,128]{2,1,0:T(8,128)} %get-tuple-element.9), custom_call_target="InvertDiagBlocksLowerTriangular" | custom-call | tf_op jit(solution)/shard_map/triangular_solve | solution.py:84
  (41 shorter events, 8.1 us)
Async XLA Ops:
  7.2 117.0 %copy-start = (bf16[1,512,1024]{2,1,0:T(8,128)(2,1)S(1)}, bf16[1,512,1024]{2,1,0:T(8,128)(2,1)}, u32[]{:S(2)}) copy-start(bf16[1,512,1024]{2,1,0:T(8,128)(2,1)} %param.7) | copy-start | bytes 3145732
  7.2 95.6 %all-gather.2.cloned.1.call-start = ((), (), s32[]{:S(2)}) async-start(), calls=%async_computation.4 | async-start | bytes 4325376 | tf_op jit(solution)/shard_map/all_gather | solution.py:43
  116.7 59.5 %all-to-all-start.1 = ((f32[8,2,32769]{2,1,0:T(2,128)}), f32[8,2,32769]{2,1,0:T(2,128)S(1)}, u32[]{:S(2)}, u32[]{:S(2)}) async-start(f32[8,2,32769]{2,1,0:T(2,128)} %pad_maximum_fusion), calls=%async_computation.1 | async-start | bytes 4210688 | tf_op jit(solution)/shard_map/all_to_all | solution.py:24
  176.2 16.3 %all-to-all-start = ((f32[8,64,256]{2,1,0:T(8,128)}), f32[8,64,256]{2,1,0:T(8,128)}, u32[]{:S(2)}, u32[]{:S(2)}) async-start(f32[8,64,256]{2,1,0:T(8,128)} %bitcast.87), calls=%async_computation | async-start | bytes 1048576 | tf_op jit(solution)/shard_map/all_to_all | solution.py:15
  192.5 35.7 %all-to-all-start.2 = ((f32[32,64,256]{2,1,0:T(8,128)}), f32[32,64,256]{2,1,0:T(8,128)S(1)}, u32[]{:S(2)}, u32[]{:S(2)}) async-start(f32[32,64,256]{2,1,0:T(8,128)} %bitcast.15), calls=%async_computation.2 | async-start | bytes 4194304 | tf_op jit(solution)/shard_map/all_to_all | solution.py:15
  230.9 29.9 %all-to-all-start.3 = ((f32[8,256,256]{2,1,0:T(8,128)}), f32[8,256,256]{2,1,0:T(8,128)S(1)}, u32[]{:S(2)}, u32[]{:S(2)}) async-start(f32[8,256,256]{2,1,0:T(8,128)} %broadcast_in_dim.39), calls=%async_computation.3 | async-start | bytes 4194304 | tf_op jit(solution)/shard_map/all_to_all | solution.py:31
Sparse Core Ops, SparseCore 0:
  9.8 92.9 all-gather.1
where the time goes:
time: 332 us; the launch traced here: 331 us
  waiting for transfers between devices  191 us (58%)
  other arithmetic  62.8 us (19%)
  local copies, waits for them, and re-layouts  25.6 us (8%)
  starting transfers between devices  23.8 us (7%)
  between operations  16.2 us (5%)
  matrix products  11.7 us (4%)
    all_gather x1, waiting for transfers between devices, on_device(): omega = lax.all_gather(samples, ('row', 'col'), axis=0, tiled=True)  90.9 us
    all_to_all x1, waiting for transfers between devices, in_one_piece(): lax.all_to_all(both, axis, split_axis=split_dim, concat_axis=concat_dim,...  47.6 us
    another operation x6, other arithmetic, on_device(): lower = jnp.linalg.cholesky(gram)  34 us
    all_to_all x1, waiting for transfers between devices, sent_to_all(): return lax.all_to_all(copies, axis, split_axis=0, concat_axis=0, tiled=True)  26.1 us
    all_to_all x2, waiting for transfers between devices, summed_on_arrival(): pieces = lax.all_to_all(in_blocks(x, dim, devices), axis, 0, 0, tiled=True)  25.7 us
    another operation x3, other arithmetic, on_device(): lax.linalg.triangular_solve(lower, masked, left_side=False, lower=True, t...  20.5 us
    all_to_all x2, starting transfers between devices, summed_on_arrival(): pieces = lax.all_to_all(in_blocks(x, dim, devices), axis, 0, 0, tiled=True)  12.4 us
    all_to_all x1, starting transfers between devices, in_one_piece(): lax.all_to_all(both, axis, split_axis=split_dim, concat_axis=concat_dim,...  7.52 us
  transfers between devices with their start and end apart: 5, of which 4 were waited for; matrix products, arithmetic and copies ran while one was open for 7% of the time, Pallas kernels for 0%

commit v1 on v0

--- a/solution.py
+++ b/solution.py
@@ -40,7 +40,10 @@
     width = samples.shape[1]
     slab = front_slab[0]
     col_width = slab.shape[1]
-    omega = lax.all_gather(samples, ("row", "col"), axis=0, tiled=True)
+    omega = jnp.concatenate(
+        lax.all_to_all(jnp.stack([samples] * lax.axis_size(("row", "col"))), ("row", "col"), 0, 0),
+        axis=0,
+    )
     full = omega.shape[0]
     own = lax.dynamic_slice_in_dim(omega, lax.axis_index("col") * col_width, col_width, 0)
     direct = summed_on_arrival(jnp.dot(slab, own, preferred_element_type=jnp.float32), "col", 0)

time: 332 us -> 288 us (0.87)
  waiting for transfers between devices: 191 us -> 147 us
  between operations: 16.2 us -> 2.87 us
  starting transfers between devices: 23.8 us -> 36.8 us
  local copies, waits for them, and re-layouts: 25.6 us -> 29.1 us
    all_gather x1 -> x0, waiting for transfers between devices: 90.9 us -> none  [on_device(): omega = lax.all_gather(samples, ('row', 'col'), axis=0, tiled=True)]
    all_to_all x0 -> x1, waiting for transfers between devices: none -> 50.8 us  [on_device(): lax.all_to_all(jnp.stack([samples] * lax.axis_size(('row', 'col'))), ('ro...]
    all_to_all x0 -> x1, starting transfers between devices: none -> 8.78 us  [on_device(): lax.all_to_all(jnp.stack([samples] * lax.axis_size(('row', 'col'))), ('ro...]
    all_to_all x2, starting transfers between devices: 12.4 us -> 16.1 us  [summed_on_arrival(): pieces = lax.all_to_all(in_blocks(x, dim, devices), axis, 0, 0, tiled=True)]
    another operation x6 -> x7, local copies, waits for them, and re-layouts: 5.27 us -> 8.73 us
    all_to_all x1, waiting for transfers between devices: 47.6 us -> 44.2 us  [in_one_piece(): lax.all_to_all(both, axis, split_axis=split_dim, concat_axis=concat_dim,...]
  transfers between devices with their start and end apart: 5 -> 5, of which waited for: 4 -> 4; matrix products, arithmetic and copies ran while one was open for 7% -> 6% of each run, Pallas kernels for 0% -> 0%
where the time goes in v1:
time: 288 us; the launch traced here: 287 us
  waiting for transfers between devices  147 us (51%)
  other arithmetic  60.1 us (21%)
  starting transfers between devices  36.8 us (13%)
  local copies, waits for them, and re-layouts  29.1 us (10%)
  matrix products  11.1 us (4%)
    all_to_all x1, waiting for transfers between devices, on_device(): lax.all_to_all(jnp.stack([samples] * lax.axis_size(('row', 'col'))), ('ro...  50.8 us
    all_to_all x1, waiting for transfers between devices, in_one_piece(): lax.all_to_all(both, axis, split_axis=split_dim, concat_axis=concat_dim,...  44.2 us
    another operation x6, other arithmetic, on_device(): lower = jnp.linalg.cholesky(gram)  34 us
    all_to_all x1, waiting for transfers between devices, sent_to_all(): return lax.all_to_all(copies, axis, split_axis=0, concat_axis=0, tiled=True)  26.1 us
    all_to_all x2, waiting for transfers between devices, summed_on_arrival(): pieces = lax.all_to_all(in_blocks(x, dim, devices), axis, 0, 0, tiled=True)  25.7 us
    another operation x3, other arithmetic, on_device(): lax.linalg.triangular_solve(lower, masked, left_side=False, lower=True, t...  20.5 us
    all_to_all x2, starting transfers between devices, summed_on_arrival(): pieces = lax.all_to_all(in_blocks(x, dim, devices), axis, 0, 0, tiled=True)  16.1 us
    all_to_all x1, starting transfers between devices, on_device(): lax.all_to_all(jnp.stack([samples] * lax.axis_size(('row', 'col'))), ('ro...  8.78 us
  transfers between devices with their start and end apart: 5, of which 4 were waited for; matrix products, arithmetic and copies ran while one was open for 6% of the time, Pallas kernels for 0%

profile of v1, /device:TPU:1, one launch (start us, length us, event | category | flops | bytes accessed | tf_op | source)
XLA Modules:
  0.0 286.9 jit_solution(10269464225098588261)
XLA Ops:
  0.6 3.4 %stack.2 = bf16[32,256,256]{2,1,0:T(8,128)(2,1)} broadcast(bf16[256,256]{1,0:T(8,128)(2,1)} %param.8), dimensions={1,2} | broadcast | bytes 4325376 | tf_op jit(solution)/shard_map/stack | solution.py:44
  4.1 8.8 %all-to-all-start = ((bf16[32,256,256]{2,1,0:T(8,128)(2,1)}), bf16[32,256,256]{2,1,0:T(8,128)(2,1)}, u32[]{:S(2)}, u32[]{:S(2)}) async-start(bf16[32,256,256]{2,1,0:T(8,128)(2,1)} %stack.2), calls=%async_computation | async-start | bytes 8388608 | tf_op jit(solution)/shard_map/all_to_all | solution.py:44
  13.6 50.8 %all-to-all-done = bf16[32,256,256]{2,1,0:T(8,128)(2,1)} async-done(((bf16[32,256,256]{2,1,0:T(8,128)(2,1)}), bf16[32,256,256]{2,1,0:T(8,128)(2,1)}, u32[]{:S(2)}, u32[]{:S(2)}) %all-to-all-start) | async-done | bytes 4194336 | tf_op jit(solution)/shard_map/all_to_all | solution.py:44
  64.4 2.9 gather_fusion
  67.3 2.1 convolution_bitcast_fusion.1
  69.6 1.2 fusion.20
  70.8 2.5 copy.28
  73.3 2.7 reshape_reshape.17
  76.0 2.3 pad_maximum_fusion
  78.3 8.2 %all-to-all-start.2 = ((f32[8,2,32769]{2,1,0:T(2,128)}), f32[8,2,32769]{2,1,0:T(2,128)S(1)}, u32[]{:S(2)}, u32[]{:S(2)}) async-start(f32[8,2,32769]{2,1,0:T(2,128)} %pad_maximum_fusion), calls=%async_computation.2 | async-start | bytes 4210688 | tf_op jit(solution)/shard_map/all_to_all | solution.py:24
  86.5 2.3 convolution_bitcast_fusion
  88.9 2.0 copy.24
  90.9 44.2 %all-to-all-done.2 = f32[8,2,32769]{2,1,0:T(2,128)S(1)} async-done(((f32[8,2,32769]{2,1,0:T(2,128)}), f32[8,2,32769]{2,1,0:T(2,128)S(1)}, u32[]{:S(2)}, u32[]{:S(2)}) %all-to-all-start.2) | async-done | bytes 2097248 | tf_op jit(solution)/shard_map/all_to_all | solution.py:24
  135.1 5.1 %all-to-all-start.1 = ((f32[8,64,256]{2,1,0:T(8,128)}), f32[8,64,256]{2,1,0:T(8,128)}, u32[]{:S(2)}, u32[]{:S(2)}) async-start(f32[8,64,256]{2,1,0:T(8,128)} %bitcast.87), calls=%async_computation.1 | async-start | bytes 1048576 | tf_op jit(solution)/shard_map/all_to_all | solution.py:15
  140.1 1.5 split.9
  141.6 4.0 %reshape_reshape.19 = f32[16,128,256]{2,1,0:T(8,128)} reshape(f32[8,2,32768]{2,1,0:T(2,128)} %split.9) | data formatting | bytes 4194304 | tf_op jit(solution)/shard_map/reshape;reshape | solution.py:77
  145.9 3.8 %fusion = f32[16,128,256]{2,0,1:T(8,128)S(1)} fusion(f32[16,128,256]{2,1,0:T(8,128)} %reshape_reshape.19, s32[16]{0:T(128)S(1)} %convert_element_type.32), kind=kOutput, calls=%fused_computation.4 | convolution fusion | flops 100663552 | bytes 4194368 | tf_op jit(solution)/shard_map/qj,qrs->jrs/dot_general | solution.py:78
  149.7 2.6 copy.31
  152.3 11.1 %all-to-all-start.3 = ((f32[32,64,256]{2,1,0:T(8,128)}), f32[32,64,256]{2,1,0:T(8,128)S(1)}, u32[]{:S(2)}, u32[]{:S(2)}) async-start(f32[32,64,256]{2,1,0:T(8,128)} %bitcast.16), calls=%async_computation.3 | async-start | bytes 4194304 | tf_op jit(solution)/shard_map/all_to_all | solution.py:15
  164.0 1.1 reduce_sum.40
  165.1 25.7 %all-to-all-done.3 = f32[32,64,256]{2,1,0:T(8,128)S(1)} async-done(((f32[32,64,256]{2,1,0:T(8,128)}), f32[32,64,256]{2,1,0:T(8,128)S(1)}, u32[]{:S(2)}, u32[]{:S(2)}) %all-to-all-start.3) | async-done | bytes 2097184 | tf_op jit(solution)/shard_map/all_to_all | solution.py:15
  192.0 1.5 broadcast_in_dim.39
  193.5 3.8 %all-to-all-start.4 = ((f32[8,256,256]{2,1,0:T(8,128)}), f32[8,256,256]{2,1,0:T(8,128)S(1)}, u32[]{:S(2)}, u32[]{:S(2)}) async-start(f32[8,256,256]{2,1,0:T(8,128)} %broadcast_in_dim.39), calls=%async_computation.4 | async-start | bytes 4194304 | tf_op jit(solution)/shard_map/all_to_all | solution.py:31
  197.3 26.1 %all-to-all-done.4 = f32[8,256,256]{2,1,0:T(8,128)S(1)} async-done(((f32[8,256,256]{2,1,0:T(8,128)}), f32[8,256,256]{2,1,0:T(8,128)S(1)}, u32[]{:S(2)}, u32[]{:S(2)}) %all-to-all-start.4) | async-done | bytes 2097184 | tf_op jit(solution)/shard_map/all_to_all | solution.py:31
  223.8 11.7 %cholesky.49 = f32[128,128]{1,0:T(8,128)S(1)} custom-call(f32[128,128]{1,0:T(8,128)S(1)} %cholesky.115), custom_call_target="Cholesky" | custom-call | tf_op jit(solution)/shard_map/jit(cholesky)/cholesky | solution.py:86
  235.6 9.8 %custom-call.14 = f32[1,128,128]{1,2,0:T(8,128)S(1)} custom-call(f32[1,128,128]{2,1,0:T(8,128)S(1)} %get-tuple-element.25), custom_call_target="InvertDiagBlocksLowerTriangular" | custom-call | tf_op jit(solution)/shard_map/jit(cholesky)/cholesky | solution.py:86
  245.9 11.7 %cholesky.103 = f32[128,128]{1,0:T(8,128)S(1)} custom-call(f32[128,128]{1,0:T(8,128)S(1)} %convolution_subtract_fusion), custom_call_target="Cholesky" | custom-call | tf_op jit(solution)/shard_map/jit(cholesky)/cholesky | solution.py:86
  257.7 0.7 compare_reduce_fusion
  259.8 5.3 %while.1 = (s32[]{:T(128)}, f32[256,256]{1,0:T(8,128)S(1)}, s32[2,2]{1,0:T(2,128)S(1)}, f32[2,128,128]{2,1,0:T(8,128)}, s32[]{:T(128)}) while((s32[]{:T(128)}, f32[256,256]{1,0:T(8,128)S(1)}, s32[2,2]{1,0:T(2,128)S(1)}, f32[2,128,128]{2,1,0:T(8,128)}, s32[]{:T(128)}) %tuple.28), condition=%wide.while_cond, body=%wide.while_body.sunk | while | flops 2 | bytes 132205 | solution.py:87
  260.4 2.0 bitcast_dynamic-update-slice_fusion.2
  263.1 2.0 bitcast_dynamic-update-slice_fusion.2
  265.1 20.5 %custom-call.15 = f32[2,128,128]{1,2,0:T(8,128)S(1)} custom-call(f32[2,128,128]{2,1,0:T(8,128)} %get-tuple-element.9), custom_call_target="InvertDiagBlocksLowerTriangular" | custom-call | tf_op jit(solution)/shard_map/triangular_solve | solution.py:87
  (47 shorter events, 5.8 us)
Async XLA Ops:
  0.6 85.9 %copy-start = (bf16[1,512,1024]{2,1,0:T(8,128)(2,1)S(1)}, bf16[1,512,1024]{2,1,0:T(8,128)(2,1)}, u32[]{:S(2)}) copy-start(bf16[1,512,1024]{2,1,0:T(8,128)(2,1)} %param.7) | copy-start | bytes 3145732
  4.1 8.8 %copy-start.2 = (s32[2,1]{0,1:T(1,128)S(1)}, s32[2,1]{0,1:T(1,128)}, u32[]{:S(2)}) copy-start(s32[2,1]{0,1:T(1,128)} %param.10) | copy-start | bytes 28
  4.1 9.1 %copy-start.3 = (s32[2]{0:T(128)S(1)}, s32[2]{0:T(128)}, u32[]{:S(2)}) copy-start(s32[2]{0:T(128)} %param.11) | copy-start | bytes 28
  4.1 9.4 %copy-start.1 = (s32[2,16]{1,0:T(2,128)S(1)}, s32[2,16]{1,0:T(2,128)}, u32[]{:S(2)}) copy-start(s32[2,16]{1,0:T(2,128)} %param.12) | copy-start | bytes 388
  4.1 60.4 %all-to-all-start = ((bf16[32,256,256]{2,1,0:T(8,128)(2,1)}), bf16[32,256,256]{2,1,0:T(8,128)(2,1)}, u32[]{:S(2)}, u32[]{:S(2)}) async-start(bf16[32,256,256]{2,1,0:T(8,128)(2,1)} %stack.2), calls=%async_computation | async-start | bytes 8388608 | tf_op jit(solution)/shard_map/all_to_all | solution.py:44
  78.3 56.7 %all-to-all-start.2 = ((f32[8,2,32769]{2,1,0:T(2,128)}), f32[8,2,32769]{2,1,0:T(2,128)S(1)}, u32[]{:S(2)}, u32[]{:S(2)}) async-start(f32[8,2,32769]{2,1,0:T(2,128)} %pad_maximum_fusion), calls=%async_computation.2 | async-start | bytes 4210688 | tf_op jit(solution)/shard_map/all_to_all | solution.py:24
  135.1 17.2 %all-to-all-start.1 = ((f32[8,64,256]{2,1,0:T(8,128)}), f32[8,64,256]{2,1,0:T(8,128)}, u32[]{:S(2)}, u32[]{:S(2)}) async-start(f32[8,64,256]{2,1,0:T(8,128)} %bitcast.87), calls=%async_computation.1 | async-start | bytes 1048576 | tf_op jit(solution)/shard_map/all_to_all | solution.py:15
  152.3 38.5 %all-to-all-start.3 = ((f32[32,64,256]{2,1,0:T(8,128)}), f32[32,64,256]{2,1,0:T(8,128)S(1)}, u32[]{:S(2)}, u32[]{:S(2)}) async-start(f32[32,64,256]{2,1,0:T(8,128)} %bitcast.16), calls=%async_computation.3 | async-start | bytes 4194304 | tf_op jit(solution)/shard_map/all_to_all | solution.py:15
  193.5 29.9 %all-to-all-start.4 = ((f32[8,256,256]{2,1,0:T(8,128)}), f32[8,256,256]{2,1,0:T(8,128)S(1)}, u32[]{:S(2)}, u32[]{:S(2)}) async-start(f32[8,256,256]{2,1,0:T(8,128)} %broadcast_in_dim.39), calls=%async_computation.4 | async-start | bytes 4194304 | tf_op jit(solution)/shard_map/all_to_all | solution.py:31
